TPU v7x, 256 devices: a whole 4x4x8 slice. The times are simulated.
256 devices in a mesh: table: 16 (over z, core), seq: 16 (over x, y).
Axes of the slice: x: 4, y: 4, z: 8, core: 2. Of those that a mesh axis runs over, the one named last changes fastest.
Arguments:
- item_ids: int32 [262144], P('seq'), may hold values from 0 to 524287, as said below
- item_table: bfloat16 [524288, 512], P('seq', 'table'), may hold values from -6 to 6
- group_counts: int32 [16, 16, 16], replicated, may hold values from 0 to 96, as said below
- lengths: int32 [16], replicated, may hold values from 128 to 512
- history: bfloat16 [16, 2, 2, 512, 512], P('table', None, None, 'seq'), may hold values from -6 to 6
- w_in: bfloat16 [512, 2048], replicated, may hold values from -0.25 to 0.25
- w_out: bfloat16 [2048, 512], replicated, may hold values from -0.125 to 0.125
- w_proj: bfloat16 [2, 512, 1024], replicated, may hold values from -0.25 to 0.25
- w_back: bfloat16 [2, 512, 512], replicated, may hold values from -0.25 to 0.25
Outputs:
- ranked_states: bfloat16 [393216, 512], P(('table', 'seq'))
Inputs may be any that keep to these rules, and one draw needn't show every extreme that they name: `item_ids`: the ids of the 16384 candidates of index s of seq lie in s * 32768 to (s + 1) * 32768 - 1. Each group_counts[t, s, :] sums to 1024; every sender has some entry equal to 96; on some index s every t sends 96 to one group.
All inputs are finite; a program needn't handle non-finite values.
Results may differ from a plain program's by a relative error of at most 0.013.
Values may be sent and summed in bfloat16 or wider, within the bound.
A program may use at most 128 MiB of HBM per device.

v0:
```python
import jax
import jax.numpy as jnp
from jax import lax
from jax.sharding import Mesh
from jax.sharding import PartitionSpec as P

HEADS = 8
HEAD_DIM = 64
SEQ = ("seq_0", "seq_1")
TABLE_SEQ = ("table", "seq_0", "seq_1")


def gather_axes(shard, axes, dim):
    if not axes:
        return shard
    nearer = lax.all_gather(shard, axes[-1], axis=dim, tiled=True)
    return gather_axes(nearer, axes[:-1], dim)


def layer_norm(values):
    row_mean = jnp.mean(values, axis=-1, keepdims=True)
    centred = values - row_mean
    variance = jnp.mean(centred * centred, axis=-1, keepdims=True)
    return centred * lax.rsqrt(variance + 1e-06)


def lookup_rows(table_shard, local_ids):
    vocab_rows = table_shard.shape[0]
    columns = table_shard.shape[1]
    packing = 1
    while columns * packing < 128 and vocab_rows % (packing * 2) == 0:
        packing = packing * 2
    packed_table = table_shard.reshape(vocab_rows // packing, columns * packing)
    wide_rows = jnp.take(packed_table, local_ids // packing, axis=0).reshape(
        local_ids.shape[0], packing, columns
    )
    chosen = (local_ids % packing)[:, None] == jnp.arange(packing, dtype=jnp.int32)[None, :]
    return jnp.sum(jnp.where(chosen[:, :, None], wide_rows, jnp.zeros((), jnp.bfloat16)), axis=1)


def content_mlp(rows_in, w_in, w_out):
    hidden = jax.nn.silu(jnp.dot(rows_in, w_in, preferred_element_type=jnp.float32)).astype(
        jnp.bfloat16
    )
    return (
        rows_in.astype(jnp.float32) + jnp.dot(hidden, w_out, preferred_element_type=jnp.float32)
    ).astype(jnp.bfloat16)


def attend_layer(states, layer_cache, key_mask, w_proj, w_back):
    row_count = states.shape[0]
    width = states.shape[1]
    normed = layer_norm(states.astype(jnp.float32)).astype(jnp.bfloat16)
    projected = jax.nn.silu(jnp.dot(normed, w_proj, preferred_element_type=jnp.float32))
    gate = projected[:, :width]
    queries = projected[:, width:].astype(jnp.bfloat16).reshape(row_count, HEADS, HEAD_DIM)
    key_heads = layer_cache[0].reshape(-1, HEADS, HEAD_DIM)
    value_heads = layer_cache[1].reshape(-1, HEADS, HEAD_DIM)
    scores = jnp.einsum(
        "qhd,khd->hqk", queries, key_heads, preferred_element_type=jnp.float32
    ) * HEAD_DIM ** (-0.5)
    weights = jnp.where(key_mask[None, None, :], jax.nn.silu(scores), 0.0).astype(jnp.bfloat16)
    attended = jnp.einsum(
        "hqk,khd->qhd", weights, value_heads, preferred_element_type=jnp.float32
    ).reshape(row_count, width)
    mixed_rows = (layer_norm(attended) * gate).astype(jnp.bfloat16)
    return (
        states.astype(jnp.float32) + jnp.dot(mixed_rows, w_back, preferred_element_type=jnp.float32)
    ).astype(jnp.bfloat16)


def local(item_ids, item_table, group_counts, lengths, history, w_in, w_out, w_proj, w_back):
    groups = lax.axis_size("table")
    shard_count = lax.axis_size(SEQ)
    table_index = lax.axis_index("table")
    seq_index = lax.axis_index(SEQ)
    vocab_rows = item_table.shape[0]
    row_count = item_ids.shape[0] // groups
    capacity = 3 * row_count // (2 * groups)
    local_ids = item_ids - seq_index * vocab_rows
    counts_here = lax.dynamic_index_in_dim(group_counts, seq_index, 1, keepdims=False)
    offsets = jnp.cumsum(counts_here, axis=1) - counts_here
    slot_ids = jnp.arange(capacity, dtype=jnp.int32)
    pieces = lookup_rows(item_table, local_ids)
    whole_rows = lax.all_to_all(pieces, "table", split_axis=0, concat_axis=1, tiled=True)
    mixed_rows = content_mlp(whole_rows, w_in, w_out)
    own_counts = lax.dynamic_index_in_dim(counts_here, table_index, 0, keepdims=False)
    own_offsets = lax.dynamic_index_in_dim(offsets, table_index, 0, keepdims=False)
    source_rows = jnp.minimum(own_offsets[:, None] + slot_ids[None, :], row_count - 1)
    filled = slot_ids[None, :] < own_counts[:, None]
    picked = jnp.take(mixed_rows, source_rows.reshape(-1), axis=0)
    outgoing = jnp.where(filled.reshape(-1, 1), picked, jnp.zeros((), jnp.bfloat16))
    states = lax.all_to_all(outgoing, "table", split_axis=0, concat_axis=0, tiled=True)
    group_length = lax.dynamic_index_in_dim(lengths, table_index, 0, keepdims=False)
    key_mask = jnp.arange(history.shape[3] * shard_count, dtype=jnp.int32) < group_length
    for layer_num in range(w_proj.shape[0]):
        layer_cache = gather_axes(history[0, layer_num], SEQ, 1)
        states = attend_layer(states, layer_cache, key_mask, w_proj[layer_num], w_back[layer_num])
    return states


def solution(mesh):
    torus = Mesh(mesh.devices.reshape(mesh.shape["table"], 4, 4), ("table", "seq_0", "seq_1"))
    in_specs = (
        P(SEQ),
        P(SEQ, "table"),
        P(),
        P(),
        P("table", None, None, SEQ, None),
        P(),
        P(),
        P(),
        P(),
    )
    out_specs = P(TABLE_SEQ, None)
    return jax.shard_map(local, mesh=torus, in_specs=in_specs, out_specs=out_specs, check_vma=False)
```

profile of v0, /device:TPU:1, one launch (start us, length us, event | category | flops | bytes accessed | tf_op | source)
XLA Modules:
  0.0 264.4 jit_solution(4371669298266426853)
XLA Ops:
  8.5 7.4 %copy.29 = bf16[32768,32]{1,0:T(8,128)(2,1)} copy(bf16[32768,32]{0,1:T(8,128)(2,1)} %param.10) | data formatting | bytes 4194304 | tf_op args[1]
  15.9 10.4 %reshape.210 = bf16[8192,128]{1,0:T(8,128)(2,1)} reshape(bf16[32768,32]{1,0:T(8,128)(2,1)} %copy.29) | data formatting | bytes 4194304 | tf_op jit(solution)/shard_map/reshape | solution.py:33
  26.3 57.2 %gather_fusion = bf16[16384,128]{1,0:T(8,128)(2,1)} fusion(bf16[8192,128]{1,0:T(8,128)(2,1)} %reshape.210, s32[16384]{0:T(1024)S(1)} %get-tuple-element.12), kind=kCustom, calls=%fused_computation | custom fusion | bytes 8454144 | tf_op jit(solution)/shard_map/jit(_take)/gather | solution.py:34
  83.5 6.4 %copy.30 = bf16[16384,128]{0,1:T(8,128)(2,1)} copy(bf16[16384,128]{1,0:T(8,128)(2,1)} %gather_fusion) | data formatting | bytes 8388608 | tf_op jit(solution)/shard_map/jit(_take)/gather | solution.py:34
  90.0 4.5 %select_reduce_fusion = bf16[16384,32]{0,1:T(8,128)(2,1)S(1)} fusion(bf16[16384,4,32]{0,2,1:T(8,128)(2,1)} %bitcast.77, pred[16384]{0:T(1024)(128)(4,1)S(1)} %compare_and_fusion, pred[16384,4]{0,1:T(4,128)(4,1)S(1)} %iota_compare_fusion), kind=kLoop, calls=%fused_computation.10 | loop fusion | flops 5767168 | bytes 5324800 | tf_op jit(solution)/shard_map/reduce_sum | solution.py:38
  95.6 10.0 %all-to-all-start = ((bf16[16,1024,32]{1,2,0:T(8,128)(2,1)}), bf16[16,1024,32]{1,2,0:T(8,128)(2,1)S(1)}, u32[]{:S(2)}, u32[]{:S(2)}) async-start(bf16[16,1024,32]{1,2,0:T(8,128)(2,1)} %bitcast.81), calls=%async_computation | async-start | bytes 2097152 | tf_op jit(solution)/shard_map/all_to_all | solution.py:85
  105.6 11.2 %all-gather = bf16[1,1,2,128,512]{4,3,2,1,0:T(8,128)(2,1)} all-gather(bf16[1,1,2,32,512]{4,3,2,1,0:T(8,128)(2,1)S(1)} %get-tuple-element.10), channel_id=2, replica_groups=mesh['table'=16,'seq_0'=4,'seq_1'=4] {'seq_1'}, dimensions={3}, use_global_device_ids=true | all-gather | bytes 327680 | tf_op jit(solution)/shard_map/all_gather | solution.py:16
  118.8 14.7 %all-to-all-done = bf16[16,1024,32]{1,2,0:T(8,128)(2,1)S(1)} async-done(((bf16[16,1024,32]{1,2,0:T(8,128)(2,1)}), bf16[16,1024,32]{1,2,0:T(8,128)(2,1)S(1)}, u32[]{:S(2)}, u32[]{:S(2)}) %all-to-all-start) | async-done | bytes 1048608 | tf_op jit(solution)/shard_map/all_to_all | solution.py:85
  134.6 1.3 copy.32
  135.9 7.6 %add_convert_fusion = bf16[1024,512]{1,0:T(8,128)(2,1)S(1)} fusion(bf16[1024,512]{1,0:T(8,128)(2,1)} %copy.32, bf16[2048,512]{1,0:T(8,128)(2,1)S(1)} %copy-done, bf16[1024,512]{0,1:T(8,128)(2,1)} %bitcast.80, bf16[512,2048]{1,0:T(8,128)(2,1)} %param.14), kind=kOutput, calls=%fused_computation.41 | convolution fusion | flops 4307025920 | bytes 7340032 | tf_op jit(solution)/shard_map/dot_general | solution.py:46
  143.5 4.8 %gather_fusion.1 = bf16[1536,512]{1,0:T(8,128)(2,1)S(1)} fusion(bf16[1024,512]{1,0:T(8,128)(2,1)S(1)} %add_convert_fusion, s32[2048]{0:T(1024)S(1)} %pad_clamp_fusion), kind=kCustom, calls=%fused_computation.1 | custom fusion | bytes 3151872 | tf_op jit(solution)/shard_map/jit(_take)/gather | solution.py:91
  148.3 1.5 select_select_fusion
  149.8 3.6 %all-to-all-start.1 = ((bf16[16,96,512]{2,1,0:T(8,128)(2,1)}), bf16[16,96,512]{2,1,0:T(8,128)(2,1)S(1)}, u32[]{:S(2)}, u32[]{:S(2)}) async-start(bf16[16,96,512]{2,1,0:T(8,128)(2,1)} %select_select_fusion), calls=%async_computation.1 | async-start | bytes 3145728 | tf_op jit(solution)/shard_map/all_to_all | solution.py:93
  153.5 11.4 %all-gather.2 = bf16[1,1,2,128,512]{4,3,2,1,0:T(8,128)(2,1)} all-gather(bf16[1,1,2,32,512]{4,3,2,1,0:T(8,128)(2,1)S(1)} %get-tuple-element.9), channel_id=4, replica_groups=mesh['table'=16,'seq_0'=4,'seq_1'=4] {'seq_1'}, dimensions={3}, use_global_device_ids=true | all-gather | bytes 327680 | tf_op jit(solution)/shard_map/all_gather | solution.py:16
  166.1 1.3 fusion.44
  169.4 22.7 %all-gather.9.cloned.1.call-done = bf16[1,1,2,512,512]{4,3,2,1,0:T(8,128)(2,1)} async-done(((bf16[1,1,2,128,512]{4,3,2,1,0:T(8,128)(2,1)}), bf16[1,1,2,512,512]{4,3,2,1,0:T(8,128)(2,1)}) %all-gather.9.cloned.1.call-update) | async-done | bytes 1048592 | tf_op jit(solution)/shard_map/all_gather | solution.py:16
  195.4 2.8 %divide_multiply_fusion.1 = f32[1536,1024]{0,1:T(8,128)S(1)} fusion(bf16[1536,512]{1,0:T(8,128)(2,1)S(1)} %bitcast.85, bf16[2,512,1024]{2,1,0:T(8,128)(2,1)S(1)} %copy-done.12), kind=kOutput, calls=%fused_computation.6 | convolution fusion | flops 1616904192 | bytes 8912896 | tf_op jit(solution)/shard_map/dot_general | solution.py:54
  198.2 2.6 %copy-done.8 = f32[1536,1024]{0,1:T(8,128)} copy-done((f32[1536,1024]{0,1:T(8,128)}, f32[1536,1024]{0,1:T(8,128)S(1)}, u32[]{:S(2)}) %copy-start.8) | copy-done | bytes 6291480
  200.9 1.3 slice.99
  202.2 13.3 %fusion.46 = (f32[1536]{0:T(1024)S(1)}, f32[8,1536,64]{1,2,0:T(8,128)}) fusion(bf16[512,8,64]{0,2,1:T(8,128)(2,1)} %bitcast.89, bf16[1536,8,64]{0,2,1:T(8,128)(2,1)} %bitcast.84, bf16[512,8,64]{0,2,1:T(8,128)(2,1)S(1)} %bitcast.88, pred[512]{0:T(512)(128)(4,1)S(1)} %iota_compare_fusion.2), kind=kOutput, calls=%fused_computation.100 | convolution fusion | flops 1655437824 | bytes 5773824 | tf_op jit(solution)/shard_map/hqk,khd->qhd/dot_general | solution.py:63
  215.5 2.4 fusion.12
  218.4 3.5 %fusion.6 = bf16[1536,512]{0,1:T(8,128)(2,1)} fusion(f32[1536,1024]{0,1:T(8,128)} %copy-done.8, f32[8,1536,64]{1,2,0:T(8,128)S(1)} %copy-done.3, f32[1536]{0:T(1024)S(1)} %add_rsqrt_fusion.2, f32[1536]{0:T(1024)S(1)} %broadcast_multiply_fusion.2), kind=kLoop, calls=%fused_computation.21 | loop fusion | flops 3145728 | bytes 7876608 | tf_op jit(solution)/shard_map/convert_element_type | solution.py:66
  221.9 2.1 copy.35
  223.9 3.7 %convert_reduce_fusion = (f32[1536]{0:T(1024)S(1)}, bf16[1536,512]{0,1:T(8,128)(2,1)S(1)}) fusion(f32[1536,512]{0,1:T(8,128)} %copy.35, bf16[1536,512]{0,1:T(8,128)(2,1)} %fusion.6, bf16[2,512,512]{2,1,0:T(8,128)(2,1)} %param.17), kind=kOutput, calls=%fused_computation.9 | convolution fusion | flops 808450560 | bytes 6821888 | tf_op jit(solution)/shard_map/dot_general | solution.py:68
  228.1 2.8 %divide_multiply_fusion = f32[1536,1024]{0,1:T(8,128)S(1)} fusion(bf16[1536,512]{0,1:T(8,128)(2,1)S(1)} %get-tuple-element.16, f32[1536]{0:T(1024)S(1)} %add_rsqrt_fusion.1, f32[1536]{0:T(1024)S(1)} %broadcast_multiply_fusion.1, bf16[2,512,1024]{2,1,0:T(8,128)(2,1)S(1)} %copy-done.13), kind=kOutput, calls=%fused_computation.5 | convolution fusion | flops 1620049920 | bytes 8929280 | tf_op jit(solution)/shard_map/dot_general | solution.py:54
  230.9 1.4 slice.98
  232.4 1.7 copy-done.7
  234.1 13.3 %fusion.47 = (f32[1536]{0:T(1024)S(1)}, f32[8,1536,64]{1,2,0:T(8,128)}) fusion(bf16[512,8,64]{0,2,1:T(8,128)(2,1)S(1)} %bitcast.87, bf16[1536,8,64]{0,2,1:T(8,128)(2,1)} %bitcast.83, bf16[512,8,64]{0,2,1:T(8,128)(2,1)S(1)} %bitcast.86, pred[512]{0:T(512)(128)(4,1)S(1)} %iota_compare_fusion.2), kind=kOutput, calls=%fused_computation.101 | convolution fusion | flops 1655437824 | bytes 5773824 | tf_op jit(solution)/shard_map/hqk,khd->qhd/dot_general | solution.py:63
  247.4 2.4 fusion.10
  250.2 2.5 fusion.5
  252.8 2.2 fusion.14
  255.0 2.6 copy.39
  (67 shorter events, 14.3 us)
Async XLA Ops:
  6.5 129.3 %copy-start = (bf16[2048,512]{1,0:T(8,128)(2,1)S(1)}, bf16[2048,512]{1,0:T(8,128)(2,1)}, u32[]{:S(2)}) copy-start(bf16[2048,512]{1,0:T(8,128)(2,1)} %param.15) | copy-start | bytes 6291460
  94.5 11.1 %copy-start.11 = (bf16[1,2,2,32,512]{4,3,2,1,0:T(8,128)(2,1)S(1)}, bf16[1,2,2,32,512]{4,3,2,1,0:T(8,128)(2,1)}, u32[]{:S(2)}) copy-start(bf16[1,2,2,32,512]{4,3,2,1,0:T(8,128)(2,1)} %param.13) | copy-start | bytes 393220
  95.6 38.0 %all-to-all-start = ((bf16[16,1024,32]{1,2,0:T(8,128)(2,1)}), bf16[16,1024,32]{1,2,0:T(8,128)(2,1)S(1)}, u32[]{:S(2)}, u32[]{:S(2)}) async-start(bf16[16,1024,32]{1,2,0:T(8,128)(2,1)} %bitcast.81), calls=%async_computation | async-start | bytes 2097152 | tf_op jit(solution)/shard_map/all_to_all | solution.py:85
  105.5 60.6 %all-gather.7.cloned.1.call-start = ((), (), s32[]{:S(2)}) async-start(), calls=%async_computation.2 | async-start | bytes 1310720 | tf_op jit(solution)/shard_map/all_gather | solution.py:16
  133.5 1.0 copy-start.6
  148.3 16.5 %copy-start.14 = (s32[16]{0:T(128)S(1)}, s32[16]{0:T(128)}, u32[]{:S(2)}) copy-start(s32[16]{0:T(128)} %param.12) | copy-start | bytes 196
  149.8 44.0 %all-to-all-start.1 = ((bf16[16,96,512]{2,1,0:T(8,128)(2,1)}), bf16[16,96,512]{2,1,0:T(8,128)(2,1)S(1)}, u32[]{:S(2)}, u32[]{:S(2)}) async-start(bf16[16,96,512]{2,1,0:T(8,128)(2,1)} %select_select_fusion), calls=%async_computation.1 | async-start | bytes 3145728 | tf_op jit(solution)/shard_map/all_to_all | solution.py:93
  153.4 38.7 %all-gather.9.cloned.1.call-start = ((), (), s32[]{:S(2)}) async-start(), calls=%async_computation.3 | async-start | bytes 1310720 | tf_op jit(solution)/shard_map/all_gather | solution.py:16
  193.8 1.6 copy-start.12
  198.2 2.7 %copy-start.8 = (f32[1536,1024]{0,1:T(8,128)}, f32[1536,1024]{0,1:T(8,128)S(1)}, u32[]{:S(2)}) copy-start(f32[1536,1024]{0,1:T(8,128)S(1)} %divide_multiply_fusion.1) | copy-start | bytes 18874372
  200.9 1.3 copy-start.9
  215.5 2.8 %copy-start.3 = (f32[8,1536,64]{1,2,0:T(8,128)S(1)}, f32[8,1536,64]{1,2,0:T(8,128)}, u32[]{:S(2)}) copy-start(f32[8,1536,64]{1,2,0:T(8,128)} %get-tuple-element.14) | copy-start | bytes 9437188
  223.9 4.2 %copy-start.13 = (bf16[2,512,1024]{2,1,0:T(8,128)(2,1)S(1)}, bf16[2,512,1024]{2,1,0:T(8,128)(2,1)}, u32[]{:S(2)}) copy-start(bf16[2,512,1024]{2,1,0:T(8,128)(2,1)} %param.16) | copy-start | bytes 6291460
  227.6 3.3 %copy-start.4 = (bf16[1536,512]{0,1:T(8,128)(2,1)}, bf16[1536,512]{0,1:T(8,128)(2,1)S(1)}, u32[]{:S(2)}) copy-start(bf16[1536,512]{0,1:T(8,128)(2,1)S(1)} %get-tuple-element.16) | copy-start | bytes 4718596
  230.9 3.1 %copy-start.7 = (f32[1536,1024]{0,1:T(8,128)}, f32[1536,1024]{0,1:T(8,128)S(1)}, u32[]{:S(2)}) copy-start(f32[1536,1024]{0,1:T(8,128)S(1)} %divide_multiply_fusion) | copy-start | bytes 18874372
  247.3 2.8 %copy-start.2 = (f32[8,1536,64]{1,2,0:T(8,128)S(1)}, f32[8,1536,64]{1,2,0:T(8,128)}, u32[]{:S(2)}) copy-start(f32[8,1536,64]{1,2,0:T(8,128)} %get-tuple-element.18) | copy-start | bytes 9437188
  250.2 2.5 copy-start.5
  250.2 2.6 copy-start.10
  252.8 4.8 %copy-start.1 = (bf16[2048,512]{1,0:T(8,128)(2,1)S(1)}, bf16[2048,512]{1,0:T(8,128)(2,1)}, u32[]{:S(2)}) copy-start(bf16[2048,512]{1,0:T(8,128)(2,1)} %param.15) | copy-start | bytes 6291460
Sparse Core Ops, SparseCore 0:
  116.9 27.2 all-gather.6
  165.0 27.0 all-gather.8
where the time goes:
time: 267 us; the launch traced here: 264 us
  local copies, waits for them, and re-layouts  110 us (41%)
  matrix products  45.7 us (17%)
  waiting for transfers between devices  37.4 us (14%)
  blocking collectives  22.6 us (8%)
  other arithmetic  21.8 us (8%)
  starting transfers between devices  13.7 us (5%)
  between operations  13.7 us (5%)
    gather x2, local copies, waits for them, and re-layouts, lookup_rows(): jnp.take(packed_table, local_ids // packing, axis=0)  63.7 us
    dot_general x2, matrix products, attend_layer(): jnp.einsum('hqk,khd->qhd', weights, value_heads, preferred_element_type=j...  26.6 us
    all_gather x2, waiting for transfers between devices, gather_axes(): nearer = lax.all_gather(shard, axes[-1], axis=dim, tiled=True)  22.7 us
    all_gather x2, blocking collectives, gather_axes(): nearer = lax.all_gather(shard, axes[-1], axis=dim, tiled=True)  22.6 us
    all_to_all x1, waiting for transfers between devices, local(): lax.all_to_all(pieces, 'table', split_axis=0, concat_axis=1, tiled=True)  14.7 us
    unnamed x31, local copies, waits for them, and re-layouts  13.8 us
    reshape x1, local copies, waits for them, and re-layouts, lookup_rows(): packed_table = table_shard.reshape(vocab_rows // packing, columns * packing)  10.4 us
    all_to_all x1, starting transfers between devices, local(): lax.all_to_all(pieces, 'table', split_axis=0, concat_axis=1, tiled=True)  9.97 us
  transfers between devices with their start and end apart: 4, of which 2 were waited for; matrix products, arithmetic and copies ran while one was open for 9% of the time, Pallas kernels for 0%

commit v1 on v0

v1 whole, which is shorter than its diff:
```python
import functools

import jax
import jax.numpy as jnp
from jax import lax
from jax.experimental import pallas as pl
from jax.experimental.pallas import tpu as pltpu
from jax.sharding import Mesh
from jax.sharding import PartitionSpec as P

HEADS = 8
HEAD_DIM = 64
SEQ = ("seq_0", "seq_1")
TABLE_SEQ = ("table", "seq_0", "seq_1")
MESH = pl.DeviceIdType.MESH
CHUNKS = 4
UNROLL = 64
NT = (((1,), (1,)), ((), ()))


def table_steps(groups):
    chips = groups // 2
    order = [chips // 2]
    for far in range(chips // 2 - 1, 0, -1):
        order += [far, chips - far]
    order.append(0)
    return [(dz, dc) for dz in order for dc in (0, 1)][:-2] + [(0, 1), (0, 0)]


def identity(size_0, size_1, dtype):
    rows = lax.broadcasted_iota(jnp.int32, (size_0, size_1), 0)
    cols = lax.broadcasted_iota(jnp.int32, (size_0, size_1), 1)
    return (rows == cols).astype(dtype)


def exchange_kernel(
    dims,
    ids_ref,
    counts_ref,
    table_ref,
    hist_ref,
    emb_ref,
    cache_ref,
    wide,
    lanes_in,
    rows,
    window,
    outgoing,
    offsets,
    load_sem,
    piece_send,
    piece_recv,
    hist_send,
    hist_recv,
    own_sem,
):
    groups, seq_0, seq_1, vocab, columns, per_sender, cap, hist_rows = dims
    table_index = lax.axis_index("table")
    x = lax.axis_index("seq_0")
    y = lax.axis_index("seq_1")
    shard = x * seq_1 + y
    chips = groups // 2
    z = table_index // 2
    core = table_index % 2
    steps = table_steps(groups)
    hops = [(dx, dy) for dx in range(seq_0) for dy in range(seq_1) if (dx, dy) != (0, 0)]
    hops.sort(key=lambda d: -(min(d[0], seq_0 - d[0]) + min(d[1], seq_1 - d[1])))

    def table_peer(dz, dc):
        return ((z + dz) % chips) * 2 + (core + dc) % 2

    load = pltpu.make_async_copy(table_ref, lanes_in, load_sem)
    load.start()
    barrier = pltpu.get_barrier_semaphore()
    for dz, dc in steps[:-1]:
        pl.semaphore_signal(barrier, inc=1, device_id={"table": table_peer(dz, dc)}, device_id_type=MESH)
    for dx, dy in hops:
        pl.semaphore_signal(
            barrier,
            inc=1,
            device_id={"seq_0": (x + dx) % seq_0, "seq_1": (y + dy) % seq_1},
            device_id_type=MESH,
        )

    def offset_row(t, carry):
        total = jnp.int32(0)
        for g in range(groups):
            offsets[t, g] = total
            total = total + counts_ref[t, shard, g]
        return carry

    lax.fori_loop(0, groups, offset_row, 0)
    pl.semaphore_wait(barrier, len(steps) - 1 + len(hops))

    cache_here = cache_ref.at[:, :, pl.ds(shard * hist_rows, hist_rows), :]
    own_hist = pltpu.make_async_copy(hist_ref, cache_here, own_sem.at[CHUNKS])
    own_hist.start()
    hist_copies = []
    for n, (dx, dy) in enumerate(hops):
        copy = pltpu.make_async_remote_copy(
            src_ref=hist_ref,
            dst_ref=cache_here,
            send_sem=hist_send.at[n],
            recv_sem=hist_recv.at[n],
            device_id={"seq_0": (x + dx) % seq_0, "seq_1": (y + dy) % seq_1},
            device_id_type=MESH,
        )
        copy.start()
        hist_copies.append(copy)

    load.wait()
    block = 256
    eye = identity(block, block, jnp.bfloat16)
    blank = jnp.zeros((128 - columns, block), jnp.bfloat16)

    def widen(b, carry):
        at = pl.multiple_of(b * block, block)
        piece = jnp.concatenate([lanes_in[:, pl.ds(at, block)], blank], axis=0)
        wide[pl.ds(at, block), :] = lax.dot_general(eye, piece, NT, preferred_element_type=jnp.float32)
        return carry

    lax.fori_loop(0, vocab // block, widen, 0)

    senders = groups // CHUNKS
    chunk_rows = senders * per_sender
    chunk_slots = senders * cap
    fold = identity(columns, 128, jnp.bfloat16)
    slot_iota = lax.broadcasted_iota(jnp.int32, (cap, 128), 0)

    def piece_copy(j, n):
        dz, dc = steps[n]
        here = emb_ref.at[pl.ds(table_index * columns, columns), pl.ds(j * chunk_slots, chunk_slots)]
        if (dz, dc) == (0, 0):
            return pltpu.make_async_copy(outgoing.at[j, n], here, own_sem.at[j])
        return pltpu.make_async_remote_copy(
            src_ref=outgoing.at[j, n],
            dst_ref=here,
            send_sem=piece_send.at[j, n],
            recv_sem=piece_recv.at[j, n],
            device_id={"table": table_peer(dz, dc)},
            device_id_type=MESH,
        )

    def chunk(j, carry):
        def take(i, inner):
            base = i * UNROLL
            for u in range(UNROLL):
                item = ids_ref[j * chunk_rows + base + u] & (vocab - 1)
                rows[pl.ds(base + u, 1), :] = wide[pl.ds(item, 1), :]
            return inner

        lax.fori_loop(0, chunk_rows // UNROLL, take, 0)
        for n, (dz, dc) in enumerate(steps):
            g = table_peer(dz, dc)
            for t in range(senders):
                sender = j * senders + t
                start = offsets[sender, g]
                filled = counts_ref[sender, shard, g]
                taken = rows[pl.ds(start + t * per_sender, cap), :]
                window[n % 2, t * cap : (t + 1) * cap, :] = jnp.where(slot_iota < filled, taken, 0.0).astype(jnp.bfloat16)
            outgoing[j, n] = lax.dot_general(
                fold, window[n % 2], NT, preferred_element_type=jnp.float32
            ).astype(jnp.bfloat16)
            piece_copy(j, n).start()
        return carry

    lax.fori_loop(0, CHUNKS, chunk, 0)

    def finish(j, carry):
        for n in range(len(steps)):
            piece_copy(j, n).wait()
        return carry

    lax.fori_loop(0, CHUNKS, finish, 0)
    for copy in hist_copies:
        copy.wait()
    own_hist.wait()


def exchange(item_ids, item_table, group_counts, history):
    groups = lax.axis_size("table")
    seq_0, seq_1 = lax.axis_size("seq_0"), lax.axis_size("seq_1")
    vocab, columns = item_table.shape
    per_sender = item_ids.shape[0] // groups
    cap = 3 * per_sender // (2 * groups)
    layers, hist_rows, width = history.shape[1], history.shape[3], history.shape[4]
    slots = groups * cap
    senders = groups // CHUNKS
    dims = (groups, seq_0, seq_1, vocab, columns, per_sender, cap, hist_rows)
    return pl.pallas_call(
        functools.partial(exchange_kernel, dims),
        out_shape=(
            jax.ShapeDtypeStruct((groups * columns, slots), jnp.bfloat16),
            jax.ShapeDtypeStruct((layers, 2, hist_rows * seq_0 * seq_1, width), jnp.bfloat16),
        ),
        in_specs=[
            pl.BlockSpec(memory_space=pltpu.SMEM),
            pl.BlockSpec(memory_space=pltpu.SMEM),
            pl.BlockSpec(memory_space=pl.ANY),
            pl.BlockSpec(memory_space=pltpu.VMEM),
        ],
        out_specs=(pl.BlockSpec(memory_space=pl.ANY), pl.BlockSpec(memory_space=pl.ANY)),
        scratch_shapes=[
            pltpu.VMEM((vocab, 128), jnp.float32),
            pltpu.VMEM((columns, vocab), jnp.bfloat16),
            pltpu.VMEM((senders * per_sender + 128, 128), jnp.float32),
            pltpu.VMEM((2, senders * cap, 128), jnp.bfloat16),
            pltpu.VMEM((CHUNKS, groups, columns, senders * cap), jnp.bfloat16),
            pltpu.SMEM((groups, groups), jnp.int32),
            pltpu.SemaphoreType.DMA,
            pltpu.SemaphoreType.DMA((CHUNKS, groups)),
            pltpu.SemaphoreType.DMA((CHUNKS, groups)),
            pltpu.SemaphoreType.DMA((seq_0 * seq_1,)),
            pltpu.SemaphoreType.DMA((seq_0 * seq_1,)),
            pltpu.SemaphoreType.DMA((CHUNKS + 1,)),
        ],
        compiler_params=pltpu.CompilerParams(
            collective_id=0, has_side_effects=True, vmem_limit_bytes=60 * 1024 * 1024
        ),
        name="exchange",
    )(item_ids, group_counts, item_table.T, history[0])


def swish(half):
    return half + half * jnp.tanh(half)


def normalize(values):
    width = values.shape[-1]
    row_mean = jnp.sum(values, axis=-1, keepdims=True) * (1.0 / width)
    centred = values - row_mean
    variance = jnp.sum(centred * centred, axis=-1, keepdims=True) * (1.0 / width)
    return centred * lax.rsqrt(variance + 1e-06)


def rank_kernel(
    block,
    lengths_ref,
    emb_hbm,
    cache_hbm,
    w_in_hbm,
    w_out_hbm,
    w_proj_hbm,
    w_back_hbm,
    out_hbm,
    emb,
    cache,
    w_in,
    w_out,
    w_proj,
    w_back,
    keys,
    vals,
    hidden,
    weights,
    out,
    sems,
    out_sems,
):
    width, slots = emb.shape
    layers = w_proj.shape[0]
    hist = cache.shape[2]
    pairs = HEADS // 2
    pair_dim = 2 * HEAD_DIM
    sources = (emb_hbm, w_in_hbm, w_out_hbm, cache_hbm, w_proj_hbm, w_back_hbm)
    targets = (emb, w_in, w_out, cache, w_proj, w_back)
    loads = [pltpu.make_async_copy(s, d, sems.at[i]) for i, (s, d) in enumerate(zip(sources, targets))]
    for load in loads:
        load.start()
    group_length = lengths_ref[lax.axis_index("table")]
    for load in loads:
        load.wait()
    low = lax.broadcasted_iota(jnp.int32, (hist, pair_dim), 1) < HEAD_DIM
    live = lax.broadcasted_iota(jnp.int32, (hist, pair_dim), 0) < group_length
    zero = jnp.zeros((), jnp.bfloat16)
    for layer in range(layers):
        for p in range(pairs):
            cols = slice(p * pair_dim, (p + 1) * pair_dim)
            key = cache[layer, 0, :, cols]
            keys[layer, 2 * p] = jnp.where(low, key, zero)
            keys[layer, 2 * p + 1] = jnp.where(low, zero, key)
            val = jnp.where(live, cache[layer, 1, :, cols], zero)
            vals[layer, p, :hist] = jnp.where(low, val, zero)
            vals[layer, p, hist:] = jnp.where(low, zero, val)
    eye = identity(block, block, jnp.bfloat16)

    def dot(a, b):
        return jnp.dot(a, b, preferred_element_type=jnp.float32)

    def out_copy(i):
        return pltpu.make_async_copy(
            out.at[pl.ds(i * block, block), :], out_hbm.at[pl.ds(i * block, block), :], out_sems.at[i]
        )

    def run(i, carry):
        at = pl.multiple_of(i * block, block)
        rows = lax.dot_general(
            eye, emb[:, pl.ds(at, block)], NT, preferred_element_type=jnp.float32
        ).astype(jnp.bfloat16)
        ff = w_in.shape[1]
        step = 512
        for f in range(0, ff, step):
            hidden[:, f : f + step] = swish(dot(rows, w_in[:, f : f + step]) * 0.5).astype(jnp.bfloat16)
        states = (rows.astype(jnp.float32) + dot(hidden[...], w_out[...])).astype(jnp.bfloat16)
        for layer in range(layers):
            normed = normalize(states.astype(jnp.float32)).astype(jnp.bfloat16)
            gate = swish(dot(normed, w_proj[layer, :, :width]) * 0.5)
            query = swish(dot(normed, w_proj[layer, :, width:]) * 0.5).astype(jnp.bfloat16) * jnp.bfloat16(1 / 16)
            attended = []
            for p in range(pairs):
                query_pair = query[:, p * pair_dim : (p + 1) * pair_dim]
                for half in range(2):
                    score = lax.dot_general(
                        query_pair, keys[layer, 2 * p + half], NT, preferred_element_type=jnp.float32
                    )
                    weights[:, half * hist : (half + 1) * hist] = swish(score.astype(jnp.bfloat16))
                attended.append(dot(weights[...], vals[layer, p]))
            mixed = (normalize(jnp.concatenate(attended, axis=1)) * gate).astype(jnp.bfloat16)
            states = (states.astype(jnp.float32) + dot(mixed, w_back[layer])).astype(jnp.bfloat16)
        out[pl.ds(at, block), :] = states
        out_copy(i).start()
        return carry

    lax.fori_loop(0, slots // block, run, 0)

    def drain(i, carry):
        out_copy(i).wait()
        return carry

    lax.fori_loop(0, slots // block, drain, 0)


def rank(lengths, emb, cache, w_in, w_out, w_proj, w_back):
    width, slots = emb.shape
    layers = w_proj.shape[0]
    hist = cache.shape[2]
    block = slots // CHUNKS
    anywhere = pl.BlockSpec(memory_space=pl.ANY)
    return pl.pallas_call(
        functools.partial(rank_kernel, block),
        out_shape=jax.ShapeDtypeStruct((slots, width), jnp.bfloat16),
        in_specs=[pl.BlockSpec(memory_space=pltpu.SMEM)] + [anywhere] * 6,
        out_specs=anywhere,
        scratch_shapes=[
            pltpu.VMEM(a.shape, a.dtype) for a in (emb, cache, w_in, w_out, w_proj, w_back)
        ]
        + [
            pltpu.VMEM((layers, HEADS, hist, 2 * HEAD_DIM), jnp.bfloat16),
            pltpu.VMEM((layers, HEADS // 2, 2 * hist, 2 * HEAD_DIM), jnp.bfloat16),
            pltpu.VMEM((block, w_in.shape[1]), jnp.bfloat16),
            pltpu.VMEM((block, 2 * hist), jnp.bfloat16),
            pltpu.VMEM((slots, width), jnp.bfloat16),
            pltpu.SemaphoreType.DMA((6,)),
            pltpu.SemaphoreType.DMA((slots // block,)),
        ],
        compiler_params=pltpu.CompilerParams(vmem_limit_bytes=60 * 1024 * 1024),
        name="rank",
    )(lengths, emb, cache, w_in, w_out, w_proj, w_back)


def local(item_ids, item_table, group_counts, lengths, history, w_in, w_out, w_proj, w_back):
    emb, cache = exchange(item_ids, item_table, group_counts, history)
    return rank(lengths, emb, cache, w_in, w_out, w_proj, w_back)


def solution(mesh):
    torus = Mesh(mesh.devices.reshape(mesh.shape["table"], 4, 4), ("table", "seq_0", "seq_1"))
    in_specs = (
        P(SEQ),
        P(SEQ, "table"),
        P(),
        P(),
        P("table", None, None, SEQ, None),
        P(),
        P(),
        P(),
        P(),
    )
    out_specs = P(TABLE_SEQ, None)
    return jax.shard_map(local, mesh=torus, in_specs=in_specs, out_specs=out_specs, check_vma=False)
```

time: 267 us -> 122 us (0.46)
  Pallas kernels: 0 us -> 121 us
  local copies, waits for them, and re-layouts: 110 us -> 0 us
  matrix products: 45.7 us -> 0 us
  waiting for transfers between devices: 37.4 us -> 0 us
  blocking collectives: 22.6 us -> 0 us
  other arithmetic: 21.8 us -> 0 us
  starting transfers between devices: 13.7 us -> 0 us
  between operations: 13.7 us -> 0.01 us
    pallas_call x0 -> x2, Pallas kernels: none -> 121 us  [the longest x1 79 us: exchange(): pl.pallas_call(functools.partial(exchange_kernel, dims), out_shape=(jax.S...]
    gather x3 -> x0, local copies, waits for them, and re-layouts: 68.5 us -> none  [the longest x2 63.7 us: lookup_rows(): jnp.take(packed_table, local_ids // packing, axis=0)]
    dot_general x7 -> x0, matrix products: 45.7 us -> none  [the longest x2 26.6 us: attend_layer(): jnp.einsum('hqk,khd->qhd', weights, value_heads, preferred_element_type=j...]
    all_gather x2 -> x0, waiting for transfers between devices: 22.7 us -> none  [gather_axes(): nearer = lax.all_gather(shard, axes[-1], axis=dim, tiled=True)]
    all_gather x2 -> x0, blocking collectives: 22.6 us -> none  [gather_axes(): nearer = lax.all_gather(shard, axes[-1], axis=dim, tiled=True)]
    all_to_all x2 -> x0, waiting for transfers between devices: 14.7 us -> none  [the longest x1 14.7 us: local(): lax.all_to_all(pieces, 'table', split_axis=0, concat_axis=1, tiled=True)]
    unnamed x31 -> x0, local copies, waits for them, and re-layouts: 13.8 us -> none
    all_to_all x2 -> x0, starting transfers between devices: 13.6 us -> none  [the longest x1 9.97 us: local(): lax.all_to_all(pieces, 'table', split_axis=0, concat_axis=1, tiled=True)]
  transfers between devices with their start and end apart: 4 -> 0, of which waited for: 2 -> 0; matrix products, arithmetic and copies ran while one was open for 9% -> 0% of each run, Pallas kernels for 0% -> 0%
where the time goes in v1:
time: 122 us; the launch traced here: 121 us
  Pallas kernels  121 us (99%)
    pallas_call x1, Pallas kernels, exchange(): pl.pallas_call(functools.partial(exchange_kernel, dims), out_shape=(jax.S...  79 us
    pallas_call x1, Pallas kernels, rank(): pl.pallas_call(functools.partial(rank_kernel, block), out_shape=jax.Shape...  42.4 us

profile of v1, /device:TPU:1, one launch (start us, length us, event | category | flops | bytes accessed | tf_op | source)
XLA Modules:
  0.0 121.5 jit_solution(13172130909631252802)
XLA Ops:
  0.0 79.0 %exchange.1 = (bf16[512,1536]{1,0:T(8,128)(2,1)}, bf16[2,2,512,512]{3,2,1,0:T(8,128)(2,1)}) custom-call(s32[16384]{0:T(1024)} %ids_ref.1, s32[16,16,16]{2,1,0:T(8,128)} %counts_ref.1, bf16[32,32768]{1,0:T(8,128)(2,1)} %bitcast.2, bf16[2,2,32,512]{3,2,1,0:T(8,128)(2,1)} %bitcast.3), custom_call_target="tpu_custom_call" | custom-call | tf_op jit(solution)/shard_map/exchange/pallas_call | solution.py:190
  79.0 42.4 %rank.1 = bf16[1536,512]{1,0:T(8,128)(2,1)} custom-call(s32[16]{0:T(128)} %lengths_ref.1, bf16[512,1536]{1,0:T(8,128)(2,1)} %get-tuple-element.7.emb_hbm, bf16[2,2,512,512]{3,2,1,0:T(8,128)(2,1)} %get-tuple-element.8.cache_hbm, bf16[512,2048]{1,0:T(8,128)(2,1)} %w_in_hbm.1, bf16[2048,512]{1,0:T(8,128)(2,1)} %w_out_hbm.1, bf16[2,512,1024]{2,1,0:T(8,128)(2,1)} %w_proj_hbm.1, ...), custom_call_target="tpu_custom_call" | custom-call | tf_op jit(solution)/shard_map/rank/pallas_call | solution.py:339

commit v2 on v0

v2 whole, which is shorter than its diff:
```python
import functools

import jax
import jax.numpy as jnp
from jax import lax
from jax.experimental import pallas as pl
from jax.experimental.pallas import tpu as pltpu
from jax.sharding import Mesh
from jax.sharding import PartitionSpec as P

HEADS = 8
HEAD_DIM = 64
SEQ = ("seq_0", "seq_1")
TABLE_SEQ = ("table", "seq_0", "seq_1")
MESH = pl.DeviceIdType.MESH
CHUNKS = 4
NT = (((1,), (1,)), ((), ()))


def table_steps(groups):
    chips = groups // 2
    order = [chips // 2]
    for far in range(chips // 2 - 1, 0, -1):
        order += [far, chips - far]
    order.append(0)
    return [(dz, dc) for dz in order for dc in (0, 1)][:-2] + [(0, 1), (0, 0)]


def identity(size_0, size_1, dtype):
    rows = lax.broadcasted_iota(jnp.int32, (size_0, size_1), 0)
    cols = lax.broadcasted_iota(jnp.int32, (size_0, size_1), 1)
    return (rows == cols).astype(dtype)


def swish(half):
    return half + half * jnp.tanh(half)


def normalize(values):
    width = values.shape[-1]
    row_mean = jnp.sum(values, axis=-1, keepdims=True) * (1.0 / width)
    centred = values - row_mean
    variance = jnp.sum(centred * centred, axis=-1, keepdims=True) * (1.0 / width)
    return centred * lax.rsqrt(variance + 1e-06)


def dot(a, b):
    return jnp.dot(a, b, preferred_element_type=jnp.float32)


def dot_nt(a, b):
    return lax.dot_general(a, b, NT, preferred_element_type=jnp.float32)


def build_caches(cache, keys, vals, group_length):
    layers, _, hist, _ = cache.shape
    pair_dim = 2 * HEAD_DIM
    low = lax.broadcasted_iota(jnp.int32, (hist, pair_dim), 1) < HEAD_DIM
    live = lax.broadcasted_iota(jnp.int32, (hist, pair_dim), 0) < group_length
    zero = jnp.zeros((), jnp.bfloat16)
    for layer in range(layers):
        for p in range(HEADS // 2):
            cols = slice(p * pair_dim, (p + 1) * pair_dim)
            key = cache[layer, 0, :, cols]
            keys[layer, 2 * p] = jnp.where(low, key, zero)
            keys[layer, 2 * p + 1] = jnp.where(low, zero, key)
            val = jnp.where(live, cache[layer, 1, :, cols], zero)
            vals[layer, p, :hist] = jnp.where(low, val, zero)
            vals[layer, p, hist:] = jnp.where(low, zero, val)


def rank_block(rows, w_in, w_out, w_proj, w_back, keys, vals, hidden, weights):
    width = rows.shape[1]
    ff = w_in.shape[1]
    hist = keys.shape[2]
    pair_dim = 2 * HEAD_DIM
    half = jnp.bfloat16(0.5)
    step = 512
    half_rows = rows * half
    for f in range(0, ff, step):
        hidden[:, f : f + step] = swish(dot(half_rows, w_in[:, f : f + step]).astype(jnp.bfloat16))
    states = (rows.astype(jnp.float32) + dot(hidden[...], w_out[...])).astype(jnp.bfloat16)
    for layer in range(w_proj.shape[0]):
        normed = normalize(states.astype(jnp.float32)).astype(jnp.bfloat16) * half
        query = swish(dot(normed, w_proj[layer, :, width:])).astype(jnp.bfloat16) * jnp.bfloat16(1 / 16)
        gate = swish(dot(normed, w_proj[layer, :, :width]))
        attended = []
        for p in range(HEADS // 2):
            query_pair = query[:, p * pair_dim : (p + 1) * pair_dim]
            for part in range(2):
                score = dot_nt(query_pair, keys[layer, 2 * p + part])
                weights[:, part * hist : (part + 1) * hist] = swish(score.astype(jnp.bfloat16))
            attended.append(dot(weights[...], vals[layer, p]))
        mixed = (normalize(jnp.concatenate(attended, axis=1)) * gate).astype(jnp.bfloat16)
        states = (states.astype(jnp.float32) + dot(mixed, w_back[layer])).astype(jnp.bfloat16)
    return states


def rank_kernel(
    dims,
    lengths_ref,
    ids_hbm,
    counts_hbm,
    table_hbm,
    hist_hbm,
    w_in_hbm,
    w_out_hbm,
    w_proj_hbm,
    w_back_hbm,
    out_hbm,
    wide,
    lanes_in,
    ids_in,
    ids_low,
    ids,
    counts,
    offsets,
    rows,
    window,
    outgoing,
    emb,
    cache,
    w_in,
    w_out,
    w_proj,
    w_back,
    keys,
    vals,
    hidden,
    weights,
    out,
    load_sem,
    weight_sem,
    piece_send,
    piece_recv,
    hist_send,
    hist_recv,
    own_sem,
    out_sem,
):
    groups, seq_0, seq_1, vocab, columns, per_sender, cap, hist_rows = dims
    table_index = lax.axis_index("table")
    x = lax.axis_index("seq_0")
    y = lax.axis_index("seq_1")
    shard = x * seq_1 + y
    chips = groups // 2
    z = table_index // 2
    core = table_index % 2
    steps = table_steps(groups)
    hops = [(dx, dy) for dx in range(seq_0) for dy in range(seq_1) if (dx, dy) != (0, 0)]
    hops.sort(key=lambda d: -(min(d[0], seq_0 - d[0]) + min(d[1], seq_1 - d[1])))
    senders = groups // CHUNKS
    chunk_rows = senders * per_sender
    chunk_slots = senders * cap

    def table_peer(dz, dc):
        return ((z + dz) % chips) * 2 + (core + dc) % 2

    cache_here = cache.at[:, :, pl.ds(shard * hist_rows, hist_rows), :]
    load_ids = pltpu.make_async_copy(ids_hbm, ids_in, load_sem.at[0])
    load_table = pltpu.make_async_copy(table_hbm, lanes_in, load_sem.at[1])
    load_counts = pltpu.make_async_copy(counts_hbm.at[:, shard, :], counts, load_sem.at[2])
    load_hist = pltpu.make_async_copy(hist_hbm, cache_here, load_sem.at[3])
    for load in (load_ids, load_table, load_counts, load_hist):
        load.start()
    sources = (w_in_hbm, w_out_hbm, w_proj_hbm, w_back_hbm)
    targets = (w_in, w_out, w_proj, w_back)
    weight_loads = [pltpu.make_async_copy(s, d, weight_sem.at[i]) for i, (s, d) in enumerate(zip(sources, targets))]
    for load in weight_loads:
        load.start()

    barrier = pltpu.get_barrier_semaphore()
    for dz, dc in steps[:-1]:
        pl.semaphore_signal(barrier, inc=1, device_id={"table": table_peer(dz, dc)}, device_id_type=MESH)
    for dx, dy in hops:
        pl.semaphore_signal(
            barrier,
            inc=1,
            device_id={"seq_0": (x + dx) % seq_0, "seq_1": (y + dy) % seq_1},
            device_id_type=MESH,
        )

    load_ids.wait()
    ids_low[...] = ids_in[...] & (vocab - 1)
    move_ids = pltpu.make_async_copy(ids_low, ids, load_sem.at[0])
    move_ids.start()
    load_table.wait()
    block = 256
    eye = identity(block, block, jnp.bfloat16)
    blank = jnp.zeros((128 - columns, block), jnp.bfloat16)

    def widen(b, carry):
        at = pl.multiple_of(b * 2 * block, 2 * block)
        piece = jnp.concatenate(
            [lanes_in[:, pl.ds(at, block)], blank, lanes_in[:, pl.ds(at + block, block)], blank], axis=0
        )
        turned = dot_nt(eye, piece)
        wide[pl.ds(at, block), :] = turned[:, :128]
        wide[pl.ds(at + block, block), :] = turned[:, 128:]
        return carry

    lax.fori_loop(0, vocab // (2 * block), widen, 0)

    load_counts.wait()

    def offset_row(t, carry):
        total = jnp.int32(0)
        for g in range(groups):
            offsets[t, g] = total
            total = total + counts[t, g]
        return carry

    lax.fori_loop(0, groups, offset_row, 0)
    load_hist.wait()
    pl.semaphore_wait(barrier, len(steps) - 1 + len(hops))

    hist_copies = []
    for n, (dx, dy) in enumerate(hops):
        copy = pltpu.make_async_remote_copy(
            src_ref=cache_here,
            dst_ref=cache_here,
            send_sem=hist_send.at[n],
            recv_sem=hist_recv.at[n],
            device_id={"seq_0": (x + dx) % seq_0, "seq_1": (y + dy) % seq_1},
            device_id_type=MESH,
        )
        copy.start()
        hist_copies.append(copy)

    fold = identity(columns, 128, jnp.bfloat16)
    slot_iota = lax.broadcasted_iota(jnp.int32, (cap, 128), 0)

    def own_copy(j):
        here = emb.at[pl.ds(table_index * columns, columns), pl.ds(j * chunk_slots, chunk_slots)]
        return pltpu.make_async_copy(outgoing.at[j, len(steps) - 1], here, own_sem.at[j])

    def piece_copy(j, n):
        dz, dc = steps[n]
        return pltpu.make_async_remote_copy(
            src_ref=outgoing.at[j, n],
            dst_ref=emb.at[pl.ds(table_index * columns, columns), pl.ds(j * chunk_slots, chunk_slots)],
            send_sem=piece_send.at[j, n],
            recv_sem=piece_recv.at[j, n],
            device_id={"table": table_peer(dz, dc)},
            device_id_type=MESH,
        )

    move_ids.wait()
    id_rows = chunk_rows // 128

    def chunk(j, carry):
        def take(i, inner):
            id_row = j * id_rows + i
            base = pl.multiple_of(i * 128, 128)
            for u in range(128):
                rows[pl.ds(base + u, 1), :] = wide[pl.ds(ids[id_row, u], 1), :]
            return inner

        lax.fori_loop(0, id_rows, take, 0)
        for n, (dz, dc) in enumerate(steps):
            g = table_peer(dz, dc)
            for t in range(senders):
                sender = j * senders + t
                start = offsets[sender, g]
                filled = counts[sender, g]
                taken = rows[pl.ds(start + t * per_sender, cap), :]
                window[n % 2, t * cap : (t + 1) * cap, :] = jnp.where(slot_iota < filled, taken, 0.0).astype(jnp.bfloat16)
            outgoing[j, n] = dot_nt(fold, window[n % 2]).astype(jnp.bfloat16)
            if n < len(steps) - 1:
                piece_copy(j, n).start()
            else:
                own_copy(j).start()
        return carry

    lax.fori_loop(0, CHUNKS, chunk, 0)

    for load in weight_loads:
        load.wait()
    for copy in hist_copies:
        copy.wait()
    build_caches(cache, keys, vals, lengths_ref[table_index])
    turn = identity(chunk_slots, chunk_slots, jnp.bfloat16)

    def out_copy(j):
        here = pl.ds(pl.multiple_of(j * chunk_slots, chunk_slots), chunk_slots)
        return pltpu.make_async_copy(out.at[here, :], out_hbm.at[here, :], out_sem.at[j])

    def run(j, carry):
        for n in range(len(steps) - 1):
            piece_copy(j, n).wait()
        own_copy(j).wait()
        at = pl.multiple_of(j * chunk_slots, chunk_slots)
        content_in = dot_nt(turn, emb[:, pl.ds(at, chunk_slots)]).astype(jnp.bfloat16)
        out[pl.ds(at, chunk_slots), :] = rank_block(
            content_in, w_in, w_out, w_proj, w_back, keys, vals, hidden, weights
        )
        out_copy(j).start()
        return carry

    lax.fori_loop(0, CHUNKS, run, 0)

    def drain(j, carry):
        out_copy(j).wait()
        return carry

    lax.fori_loop(0, CHUNKS, drain, 0)


def local(item_ids, item_table, group_counts, lengths, history, w_in, w_out, w_proj, w_back):
    groups = lax.axis_size("table")
    seq_0, seq_1 = lax.axis_size("seq_0"), lax.axis_size("seq_1")
    vocab, columns = item_table.shape
    per_sender = item_ids.shape[0] // groups
    cap = 3 * per_sender // (2 * groups)
    layers, hist_rows, width = history.shape[1], history.shape[3], history.shape[4]
    hist = hist_rows * seq_0 * seq_1
    slots = groups * cap
    senders = groups // CHUNKS
    block = senders * cap
    dims = (groups, seq_0, seq_1, vocab, columns, per_sender, cap, hist_rows)
    id_rows = item_ids.shape[0] // 128
    anywhere = pl.BlockSpec(memory_space=pl.ANY)
    vmem, dma = pltpu.VMEM, pltpu.SemaphoreType.DMA
    return pl.pallas_call(
        functools.partial(rank_kernel, dims),
        out_shape=jax.ShapeDtypeStruct((slots, width), jnp.bfloat16),
        in_specs=[pl.BlockSpec(memory_space=pltpu.SMEM)] + [anywhere] * 8,
        out_specs=anywhere,
        scratch_shapes=[
            vmem((vocab, 128), jnp.float32),
            vmem((columns, vocab), jnp.bfloat16),
            vmem((id_rows, 128), jnp.int32),
            vmem((id_rows, 128), jnp.int32),
            pltpu.SMEM((id_rows, 128), jnp.int32),
            pltpu.SMEM((groups, groups), jnp.int32),
            pltpu.SMEM((groups, groups), jnp.int32),
            vmem((senders * per_sender + 128, 128), jnp.float32),
            vmem((2, block, 128), jnp.bfloat16),
            vmem((CHUNKS, groups, columns, block), jnp.bfloat16),
            vmem((width, slots), jnp.bfloat16),
            vmem((layers, 2, hist, width), jnp.bfloat16),
            vmem(w_in.shape, jnp.bfloat16),
            vmem(w_out.shape, jnp.bfloat16),
            vmem(w_proj.shape, jnp.bfloat16),
            vmem(w_back.shape, jnp.bfloat16),
            vmem((layers, HEADS, hist, 2 * HEAD_DIM), jnp.bfloat16),
            vmem((layers, HEADS // 2, 2 * hist, 2 * HEAD_DIM), jnp.bfloat16),
            vmem((block, w_in.shape[1]), jnp.bfloat16),
            vmem((block, 2 * hist), jnp.bfloat16),
            vmem((slots, width), jnp.bfloat16),
            dma((4,)),
            dma((4,)),
            dma((CHUNKS, groups)),
            dma((CHUNKS, groups)),
            dma((seq_0 * seq_1,)),
            dma((seq_0 * seq_1,)),
            dma((CHUNKS,)),
            dma((CHUNKS,)),
        ],
        compiler_params=pltpu.CompilerParams(
            collective_id=0, has_side_effects=True, vmem_limit_bytes=62 * 1024 * 1024
        ),
        name="rank",
    )(lengths, item_ids.reshape(id_rows, 128), group_counts, item_table.T, history[0], w_in, w_out, w_proj, w_back)


def solution(mesh):
    torus = Mesh(mesh.devices.reshape(mesh.shape["table"], 4, 4), ("table", "seq_0", "seq_1"))
    in_specs = (
        P(SEQ),
        P(SEQ, "table"),
        P(),
        P(),
        P("table", None, None, SEQ, None),
        P(),
        P(),
        P(),
        P(),
    )
    out_specs = P(TABLE_SEQ, None)
    return jax.shard_map(local, mesh=torus, in_specs=in_specs, out_specs=out_specs, check_vma=False)
```

time: 267 us -> 87.3 us (0.33)
  the two profiles are of different devices: /device:TPU:1 before, /device:TPU:4 now
where the time goes in v2:
time: 87.3 us; the launch traced here: 87.2 us
  Pallas kernels  84.5 us (97%)
  local copies, waits for them, and re-layouts  2.65 us (3%)
    pallas_call x1, Pallas kernels, local(): pl.pallas_call(functools.partial(rank_kernel, dims), out_shape=jax.ShapeD...  84.5 us
    unnamed x1, local copies, waits for them, and re-layouts  2.65 us

profile of v2, /device:TPU:4, one launch (start us, length us, event | category | flops | bytes accessed | tf_op | source)
XLA Modules:
  0.0 87.2 jit_solution(10135794187306328101)
XLA Ops:
  0.0 84.5 %rank.1 = bf16[1536,512]{1,0:T(8,128)(2,1)} custom-call(s32[16]{0:T(128)} %lengths_ref.1, s32[128,128]{1,0:T(8,128)} %bitcast.5, s32[16,16,16]{2,1,0:T(8,128)} %counts_hbm.1, bf16[32,32768]{1,0:T(8,128)(2,1)} %bitcast.3, bf16[2,2,32,512]{3,2,1,0:T(8,128)(2,1)} %bitcast.4, bf16[512,2048]{1,0:T(8,128)(2,1)} %w_in_hbm.1, bf16[2048,512]{1,0:T(8,128)(2,1)} %w_out_hbm.1, ...), custom_call_target="tpu_custom_call" | custom-call | tf_op jit(solution)/shard_map/rank/pallas_call | solution.py:324
  84.5 2.7 %copy.11 = bf16[1536,512]{1,0:T(8,128)(2,1)} copy(bf16[1536,512]{1,0:T(8,128)(2,1)} %rank.1) | data formatting | bytes 3145728

commit v3 on v2

--- a/solution.py
+++ b/solution.py
@@ -14,6 +14,7 @@
 TABLE_SEQ = ("table", "seq_0", "seq_1")
 MESH = pl.DeviceIdType.MESH
 CHUNKS = 4
+TAKE = 8
 NT = (((1,), (1,)), ((), ()))
 
 
@@ -53,7 +54,8 @@
 
 
 def build_caches(cache, keys, vals, group_length):
-    layers, _, hist, _ = cache.shape
+    layers, _, seq_0, part, _ = cache.shape
+    hist = seq_0 * part
     pair_dim = 2 * HEAD_DIM
     low = lax.broadcasted_iota(jnp.int32, (hist, pair_dim), 1) < HEAD_DIM
     live = lax.broadcasted_iota(jnp.int32, (hist, pair_dim), 0) < group_length
@@ -61,10 +63,10 @@
     for layer in range(layers):
         for p in range(HEADS // 2):
             cols = slice(p * pair_dim, (p + 1) * pair_dim)
-            key = cache[layer, 0, :, cols]
+            key = cache[layer, 0, :, :, cols].reshape(hist, pair_dim)
             keys[layer, 2 * p] = jnp.where(low, key, zero)
             keys[layer, 2 * p + 1] = jnp.where(low, zero, key)
-            val = jnp.where(live, cache[layer, 1, :, cols], zero)
+            val = jnp.where(live, cache[layer, 1, :, :, cols].reshape(hist, pair_dim), zero)
             vals[layer, p, :hist] = jnp.where(low, val, zero)
             vals[layer, p, hist:] = jnp.where(low, zero, val)
 
@@ -98,7 +100,7 @@
 
 def rank_kernel(
     dims,
-    lengths_ref,
+    lengths_hbm,
     ids_hbm,
     counts_hbm,
     table_hbm,
@@ -107,13 +109,14 @@
     w_out_hbm,
     w_proj_hbm,
     w_back_hbm,
-    out_hbm,
+    out,
     wide,
     lanes_in,
     ids_in,
     ids_low,
     ids,
     counts,
+    lengths,
     offsets,
     rows,
     window,
@@ -128,7 +131,6 @@
     vals,
     hidden,
     weights,
-    out,
     load_sem,
     weight_sem,
     piece_send,
@@ -136,7 +138,6 @@
     hist_send,
     hist_recv,
     own_sem,
-    out_sem,
 ):
     groups, seq_0, seq_1, vocab, columns, per_sender, cap, hist_rows = dims
     table_index = lax.axis_index("table")
@@ -147,8 +148,8 @@
     z = table_index // 2
     core = table_index % 2
     steps = table_steps(groups)
-    hops = [(dx, dy) for dx in range(seq_0) for dy in range(seq_1) if (dx, dy) != (0, 0)]
-    hops.sort(key=lambda d: -(min(d[0], seq_0 - d[0]) + min(d[1], seq_1 - d[1])))
+    x_far = sorted(range(1, seq_0), key=lambda d: -min(d, seq_0 - d))
+    y_far = sorted(range(1, seq_1), key=lambda d: -min(d, seq_1 - d))
     senders = groups // CHUNKS
     chunk_rows = senders * per_sender
     chunk_slots = senders * cap
@@ -156,35 +157,33 @@
     def table_peer(dz, dc):
         return ((z + dz) % chips) * 2 + (core + dc) % 2
 
-    cache_here = cache.at[:, :, pl.ds(shard * hist_rows, hist_rows), :]
+    mine = pl.ds(y * hist_rows, hist_rows)
     load_ids = pltpu.make_async_copy(ids_hbm, ids_in, load_sem.at[0])
     load_table = pltpu.make_async_copy(table_hbm, lanes_in, load_sem.at[1])
     load_counts = pltpu.make_async_copy(counts_hbm.at[:, shard, :], counts, load_sem.at[2])
-    load_hist = pltpu.make_async_copy(hist_hbm, cache_here, load_sem.at[3])
-    for load in (load_ids, load_table, load_counts, load_hist):
+    load_hist = pltpu.make_async_copy(hist_hbm, cache.at[:, :, x, mine, :], load_sem.at[3])
+    load_lengths = pltpu.make_async_copy(lengths_hbm, lengths, load_sem.at[4])
+    for load in (load_ids, load_table, load_counts, load_hist, load_lengths):
         load.start()
     sources = (w_in_hbm, w_out_hbm, w_proj_hbm, w_back_hbm)
     targets = (w_in, w_out, w_proj, w_back)
     weight_loads = [pltpu.make_async_copy(s, d, weight_sem.at[i]) for i, (s, d) in enumerate(zip(sources, targets))]
-    for load in weight_loads:
-        load.start()
 
     barrier = pltpu.get_barrier_semaphore()
     for dz, dc in steps[:-1]:
         pl.semaphore_signal(barrier, inc=1, device_id={"table": table_peer(dz, dc)}, device_id_type=MESH)
-    for dx, dy in hops:
-        pl.semaphore_signal(
-            barrier,
-            inc=1,
-            device_id={"seq_0": (x + dx) % seq_0, "seq_1": (y + dy) % seq_1},
-            device_id_type=MESH,
-        )
+    for d in x_far:
+        pl.semaphore_signal(barrier, inc=1, device_id={"seq_0": (x + d) % seq_0}, device_id_type=MESH)
+    for d in y_far:
+        pl.semaphore_signal(barrier, inc=1, device_id={"seq_1": (y + d) % seq_1}, device_id_type=MESH)
 
     load_ids.wait()
     ids_low[...] = ids_in[...] & (vocab - 1)
     move_ids = pltpu.make_async_copy(ids_low, ids, load_sem.at[0])
     move_ids.start()
     load_table.wait()
+    for load in weight_loads:
+        load.start()
     block = 256
     eye = identity(block, block, jnp.bfloat16)
     blank = jnp.zeros((128 - columns, block), jnp.bfloat16)
@@ -202,6 +201,7 @@
     lax.fori_loop(0, vocab // (2 * block), widen, 0)
 
     load_counts.wait()
+    load_lengths.wait()
 
     def offset_row(t, carry):
         total = jnp.int32(0)
@@ -212,20 +212,33 @@
 
     lax.fori_loop(0, groups, offset_row, 0)
     load_hist.wait()
-    pl.semaphore_wait(barrier, len(steps) - 1 + len(hops))
-
-    hist_copies = []
-    for n, (dx, dy) in enumerate(hops):
-        copy = pltpu.make_async_remote_copy(
-            src_ref=cache_here,
-            dst_ref=cache_here,
+    pl.semaphore_wait(barrier, len(steps) - 1 + len(x_far) + len(y_far))
+
+    def hist_copy(n, view, axis, to):
+        return pltpu.make_async_remote_copy(
+            src_ref=view,
+            dst_ref=view,
             send_sem=hist_send.at[n],
             recv_sem=hist_recv.at[n],
-            device_id={"seq_0": (x + dx) % seq_0, "seq_1": (y + dy) % seq_1},
+            device_id={axis: to},
             device_id_type=MESH,
         )
+
+    own_keys = cache.at[:, 0, x, mine, :]
+    own_vals = cache.at[:, 1, x, mine, :]
+    row_keys = cache.at[:, 0, x, :, :]
+    row_vals = cache.at[:, 1, :, mine, :]
+    first, second = [], []
+    for d in y_far:
+        first.append(hist_copy(len(first), own_keys, "seq_1", (y + d) % seq_1))
+    for d in x_far:
+        first.append(hist_copy(len(first), own_vals, "seq_0", (x + d) % seq_0))
+    for d in x_far:
+        second.append(hist_copy(len(first) + len(second), row_keys, "seq_0", (x + d) % seq_0))
+    for d in y_far:
+        second.append(hist_copy(len(first) + len(second), row_vals, "seq_1", (y + d) % seq_1))
+    for copy in first:
         copy.start()
-        hist_copies.append(copy)
 
     fold = identity(columns, 128, jnp.bfloat16)
     slot_iota = lax.broadcasted_iota(jnp.int32, (cap, 128), 0)
@@ -247,13 +260,15 @@
 
     move_ids.wait()
     id_rows = chunk_rows // 128
+    places = [table_index // groups + u for u in range(TAKE)]
 
     def chunk(j, carry):
         def take(i, inner):
-            id_row = j * id_rows + i
-            base = pl.multiple_of(i * 128, 128)
-            for u in range(128):
-                rows[pl.ds(base + u, 1), :] = wide[pl.ds(ids[id_row, u], 1), :]
+            for v in range(128 // TAKE):
+                some = ids.at[j * id_rows + i, pl.ds(v * TAKE, TAKE)]
+                into = rows.at[pl.ds(pl.multiple_of(i * 128 + v * TAKE, TAKE), TAKE), :]
+                for u in range(TAKE):
+                    into[u : u + 1, :] = wide[pl.ds(some[places[u]], 1), :]
             return inner
 
         lax.fori_loop(0, id_rows, take, 0)
@@ -270,20 +285,24 @@
                 piece_copy(j, n).start()
             else:
                 own_copy(j).start()
+
+        @pl.when(j == 0)
+        def _():
+            for copy in first:
+                copy.wait()
+            for copy in second:
+                copy.start()
+
         return carry
 
     lax.fori_loop(0, CHUNKS, chunk, 0)
 
     for load in weight_loads:
         load.wait()
-    for copy in hist_copies:
+    for copy in second:
         copy.wait()
-    build_caches(cache, keys, vals, lengths_ref[table_index])
+    build_caches(cache, keys, vals, lengths[table_index])
     turn = identity(chunk_slots, chunk_slots, jnp.bfloat16)
-
-    def out_copy(j):
-        here = pl.ds(pl.multiple_of(j * chunk_slots, chunk_slots), chunk_slots)
-        return pltpu.make_async_copy(out.at[here, :], out_hbm.at[here, :], out_sem.at[j])
 
     def run(j, carry):
         for n in range(len(steps) - 1):
@@ -294,16 +313,9 @@
         out[pl.ds(at, chunk_slots), :] = rank_block(
             content_in, w_in, w_out, w_proj, w_back, keys, vals, hidden, weights
         )
-        out_copy(j).start()
         return carry
 
     lax.fori_loop(0, CHUNKS, run, 0)
-
-    def drain(j, carry):
-        out_copy(j).wait()
-        return carry
-
-    lax.fori_loop(0, CHUNKS, drain, 0)
 
 
 def local(item_ids, item_table, group_counts, lengths, history, w_in, w_out, w_proj, w_back):
@@ -319,13 +331,15 @@
     block = senders * cap
     dims = (groups, seq_0, seq_1, vocab, columns, per_sender, cap, hist_rows)
     id_rows = item_ids.shape[0] // 128
-    anywhere = pl.BlockSpec(memory_space=pl.ANY)
+    in_hbm = pl.BlockSpec(memory_space=pltpu.HBM)
     vmem, dma = pltpu.VMEM, pltpu.SemaphoreType.DMA
+    operands = (lengths, item_ids.reshape(id_rows, 128), group_counts, item_table.T, history[0], w_in, w_out, w_proj, w_back)
+    operands = [pltpu.with_memory_space_constraint(a, pltpu.HBM) for a in operands]
     return pl.pallas_call(
         functools.partial(rank_kernel, dims),
         out_shape=jax.ShapeDtypeStruct((slots, width), jnp.bfloat16),
-        in_specs=[pl.BlockSpec(memory_space=pltpu.SMEM)] + [anywhere] * 8,
-        out_specs=anywhere,
+        in_specs=[in_hbm] * 9,
+        out_specs=pl.BlockSpec(memory_space=pltpu.VMEM),
         scratch_shapes=[
             vmem((vocab, 128), jnp.float32),
             vmem((columns, vocab), jnp.bfloat16),
@@ -333,12 +347,13 @@
             vmem((id_rows, 128), jnp.int32),
             pltpu.SMEM((id_rows, 128), jnp.int32),
             pltpu.SMEM((groups, groups), jnp.int32),
+            pltpu.SMEM((groups,), jnp.int32),
             pltpu.SMEM((groups, groups), jnp.int32),
             vmem((senders * per_sender + 128, 128), jnp.float32),
             vmem((2, block, 128), jnp.bfloat16),
             vmem((CHUNKS, groups, columns, block), jnp.bfloat16),
             vmem((width, slots), jnp.bfloat16),
-            vmem((layers, 2, hist, width), jnp.bfloat16),
+            vmem((layers, 2, seq_0, seq_1 * hist_rows, width), jnp.bfloat16),
             vmem(w_in.shape, jnp.bfloat16),
             vmem(w_out.shape, jnp.bfloat16),
             vmem(w_proj.shape, jnp.bfloat16),
@@ -347,21 +362,19 @@
             vmem((layers, HEADS // 2, 2 * hist, 2 * HEAD_DIM), jnp.bfloat16),
             vmem((block, w_in.shape[1]), jnp.bfloat16),
             vmem((block, 2 * hist), jnp.bfloat16),
-            vmem((slots, width), jnp.bfloat16),
-            dma((4,)),
+            dma((5,)),
             dma((4,)),
             dma((CHUNKS, groups)),
             dma((CHUNKS, groups)),
-            dma((seq_0 * seq_1,)),
-            dma((seq_0 * seq_1,)),
-            dma((CHUNKS,)),
+            dma((2 * (seq_0 + seq_1 - 2),)),
+            dma((2 * (seq_0 + seq_1 - 2),)),
             dma((CHUNKS,)),
         ],
         compiler_params=pltpu.CompilerParams(
-            collective_id=0, has_side_effects=True, vmem_limit_bytes=62 * 1024 * 1024
+            collective_id=0, has_side_effects=True, vmem_limit_bytes=50 * 1024 * 1024
         ),
         name="rank",
-    )(lengths, item_ids.reshape(id_rows, 128), group_counts, item_table.T, history[0], w_in, w_out, w_proj, w_back)
+    )(*operands)
 
 
 def solution(mesh):

time: 87.3 us -> 76.9 us (0.88)
  the two profiles are of different devices: /device:TPU:4 before, /device:TPU:1 now
where the time goes in v3:
time: 76.9 us; the launch traced here: 76.8 us
  Pallas kernels  75.6 us (98%)
  local copies, waits for them, and re-layouts  1.15 us (1%)
    pallas_call x1, Pallas kernels, local(): pl.pallas_call(functools.partial(rank_kernel, dims), out_shape=jax.ShapeD...  75.6 us

profile of v3, /device:TPU:1, one launch (start us, length us, event | category | flops | bytes accessed | tf_op | source)
XLA Modules:
  0.0 76.8 jit_solution(9378770278468546038)
XLA Ops:
  0.0 75.6 %rank.1 = bf16[1536,512]{1,0:T(8,128)(2,1)S(1)} custom-call(s32[16]{0:T(128)} %lengths_hbm.1, s32[128,128]{1,0:T(8,128)} %bitcast.5, s32[16,16,16]{2,1,0:T(8,128)} %counts_hbm.1, bf16[32,32768]{1,0:T(8,128)(2,1)} %bitcast.3, bf16[2,2,32,512]{3,2,1,0:T(8,128)(2,1)} %bitcast.4, bf16[512,2048]{1,0:T(8,128)(2,1)} %w_in_hbm.1, bf16[2048,512]{1,0:T(8,128)(2,1)} %w_out_hbm.1, ...), custom_call_target="tpu_custom_call" | custom-call | tf_op jit(solution)/shard_map/rank/pallas_call | solution.py:338
  75.6 1.1 %copy.11 = bf16[1536,512]{1,0:T(8,128)(2,1)} copy(bf16[1536,512]{1,0:T(8,128)(2,1)S(1)} %rank.1) | data formatting | bytes 3145728

commit v4 on v3

--- a/solution.py
+++ b/solution.py
@@ -15,6 +15,7 @@
 MESH = pl.DeviceIdType.MESH
 CHUNKS = 4
 TAKE = 8
+PARTS = 2
 NT = (((1,), (1,)), ((), ()))
 
 
@@ -71,31 +72,52 @@
             vals[layer, p, hist:] = jnp.where(low, zero, val)
 
 
-def rank_block(rows, w_in, w_out, w_proj, w_back, keys, vals, hidden, weights):
-    width = rows.shape[1]
+def content_block(rows, w_in, w_out, hidden):
     ff = w_in.shape[1]
+    step = 512
+    half_rows = rows * jnp.bfloat16(0.5)
+    for f in range(0, ff, step):
+        hidden[:, f : f + step] = swish(dot(half_rows, w_in[:, f : f + step]).astype(jnp.bfloat16))
+    return (rows.astype(jnp.float32) + dot(hidden[...], w_out[...])).astype(jnp.bfloat16)
+
+
+def layers_block(states, w_proj, w_back, keys, vals, weights):
+    rows, width = states.shape
     hist = keys.shape[2]
     pair_dim = 2 * HEAD_DIM
-    half = jnp.bfloat16(0.5)
-    step = 512
-    half_rows = rows * half
-    for f in range(0, ff, step):
-        hidden[:, f : f + step] = swish(dot(half_rows, w_in[:, f : f + step]).astype(jnp.bfloat16))
-    states = (rows.astype(jnp.float32) + dot(hidden[...], w_out[...])).astype(jnp.bfloat16)
+    pairs = HEADS // 2
+    cut = rows // PARTS
+    side = width // 2
+    parts = [states[k * cut : (k + 1) * cut] for k in range(PARTS)]
     for layer in range(w_proj.shape[0]):
-        normed = normalize(states.astype(jnp.float32)).astype(jnp.bfloat16) * half
-        query = swish(dot(normed, w_proj[layer, :, width:])).astype(jnp.bfloat16) * jnp.bfloat16(1 / 16)
-        gate = swish(dot(normed, w_proj[layer, :, :width]))
-        attended = []
-        for p in range(HEADS // 2):
+        queries, gates = [], []
+        for part in parts:
+            normed = normalize(part.astype(jnp.float32)).astype(jnp.bfloat16) * jnp.bfloat16(0.5)
+            queries.append(swish(dot(normed, w_proj[layer, :, width:])).astype(jnp.bfloat16) * jnp.bfloat16(1 / 16))
+            gates.append(swish(dot(normed, w_proj[layer, :, :width])))
+        query = jnp.concatenate(queries, axis=0)
+        attended = [[] for _ in parts]
+        for p in range(pairs):
             query_pair = query[:, p * pair_dim : (p + 1) * pair_dim]
-            for part in range(2):
-                score = dot_nt(query_pair, keys[layer, 2 * p + part])
-                weights[:, part * hist : (part + 1) * hist] = swish(score.astype(jnp.bfloat16))
-            attended.append(dot(weights[...], vals[layer, p]))
-        mixed = (normalize(jnp.concatenate(attended, axis=1)) * gate).astype(jnp.bfloat16)
-        states = (states.astype(jnp.float32) + dot(mixed, w_back[layer])).astype(jnp.bfloat16)
-    return states
+            for head in range(2):
+                score = dot_nt(query_pair, keys[layer, 2 * p + head])
+                weights[p % 2, head] = swish(score.astype(jnp.bfloat16))
+            value = [vals[layer, p, head * hist : (head + 1) * hist] for head in range(2)]
+            if p < pairs - 1:
+                both = dot(weights[p % 2, 0], value[0]) + dot(weights[p % 2, 1], value[1])
+                for k in range(PARTS):
+                    attended[k].append(both[k * cut : (k + 1) * cut])
+            else:
+                for k in range(PARTS):
+                    own = slice(k * cut, (k + 1) * cut)
+                    attended[k].append(dot(weights[p % 2, 0, own], value[0]) + dot(weights[p % 2, 1, own], value[1]))
+        after = []
+        for part, pieces, gate in zip(parts, attended, gates):
+            mixed = (normalize(jnp.concatenate(pieces, axis=1)) * gate).astype(jnp.bfloat16)
+            back = [dot(mixed, w_back[layer, :, c : c + side]) for c in range(0, width, side)]
+            after.append((part.astype(jnp.float32) + jnp.concatenate(back, axis=1)).astype(jnp.bfloat16))
+        parts = after
+    return jnp.concatenate(parts, axis=0)
 
 
 def rank_kernel(
@@ -299,20 +321,29 @@
 
     for load in weight_loads:
         load.wait()
+    turn = identity(chunk_slots, chunk_slots, jnp.bfloat16)
+
+    def block_rows(j):
+        return pl.ds(pl.multiple_of(j * chunk_slots, chunk_slots), chunk_slots)
+
+    def content(j):
+        for n in range(len(steps) - 1):
+            piece_copy(j, n).wait()
+        own_copy(j).wait()
+        content_in = dot_nt(turn, emb[:, block_rows(j)]).astype(jnp.bfloat16)
+        out[block_rows(j), :] = content_block(content_in, w_in, w_out, hidden)
+
+    content(0)
     for copy in second:
         copy.wait()
     build_caches(cache, keys, vals, lengths[table_index])
-    turn = identity(chunk_slots, chunk_slots, jnp.bfloat16)
 
     def run(j, carry):
-        for n in range(len(steps) - 1):
-            piece_copy(j, n).wait()
-        own_copy(j).wait()
-        at = pl.multiple_of(j * chunk_slots, chunk_slots)
-        content_in = dot_nt(turn, emb[:, pl.ds(at, chunk_slots)]).astype(jnp.bfloat16)
-        out[pl.ds(at, chunk_slots), :] = rank_block(
-            content_in, w_in, w_out, w_proj, w_back, keys, vals, hidden, weights
-        )
+        @pl.when(j > 0)
+        def _():
+            content(j)
+
+        out[block_rows(j), :] = layers_block(out[block_rows(j), :], w_proj, w_back, keys, vals, weights)
         return carry
 
     lax.fori_loop(0, CHUNKS, run, 0)
@@ -361,7 +392,7 @@
             vmem((layers, HEADS, hist, 2 * HEAD_DIM), jnp.bfloat16),
             vmem((layers, HEADS // 2, 2 * hist, 2 * HEAD_DIM), jnp.bfloat16),
             vmem((block, w_in.shape[1]), jnp.bfloat16),
-            vmem((block, 2 * hist), jnp.bfloat16),
+            vmem((2, 2, block, hist), jnp.bfloat16),
             dma((5,)),
             dma((4,)),
             dma((CHUNKS, groups)),

time: 76.9 us -> 73.6 us (0.957)
  Pallas kernels: 75.6 us -> 72.4 us
    pallas_call x1, Pallas kernels: 75.6 us -> 72.4 us  [local(): pl.pallas_call(functools.partial(rank_kernel, dims), out_shape=jax.ShapeD...]
where the time goes in v4:
time: 73.6 us; the launch traced here: 73.5 us
  Pallas kernels  72.4 us (98%)
  local copies, waits for them, and re-layouts  1.15 us (2%)
    pallas_call x1, Pallas kernels, local(): pl.pallas_call(functools.partial(rank_kernel, dims), out_shape=jax.ShapeD...  72.4 us

profile of v4, /device:TPU:1, one launch (start us, length us, event | category | flops | bytes accessed | tf_op | source)
XLA Modules:
  0.0 73.5 jit_solution(11414664106963870191)
XLA Ops:
  0.0 72.4 %rank.1 = bf16[1536,512]{1,0:T(8,128)(2,1)S(1)} custom-call(s32[16]{0:T(128)} %lengths_hbm.1, s32[128,128]{1,0:T(8,128)} %bitcast.5, s32[16,16,16]{2,1,0:T(8,128)} %counts_hbm.1, bf16[32,32768]{1,0:T(8,128)(2,1)} %bitcast.3, bf16[2,2,32,512]{3,2,1,0:T(8,128)(2,1)} %bitcast.4, bf16[512,2048]{1,0:T(8,128)(2,1)} %w_in_hbm.1, bf16[2048,512]{1,0:T(8,128)(2,1)} %w_out_hbm.1, ...), custom_call_target="tpu_custom_call" | custom-call | tf_op jit(solution)/shard_map/rank/pallas_call | solution.py:369
  72.4 1.1 %copy.11 = bf16[1536,512]{1,0:T(8,128)(2,1)} copy(bf16[1536,512]{1,0:T(8,128)(2,1)S(1)} %rank.1) | data formatting | bytes 3145728

commit v5 on v4

--- a/solution.py
+++ b/solution.py
@@ -16,6 +16,7 @@
 CHUNKS = 4
 TAKE = 8
 PARTS = 2
+WIDEN = 4
 NT = (((1,), (1,)), ((), ()))
 
 
@@ -211,16 +212,17 @@
     blank = jnp.zeros((128 - columns, block), jnp.bfloat16)
 
     def widen(b, carry):
-        at = pl.multiple_of(b * 2 * block, 2 * block)
-        piece = jnp.concatenate(
-            [lanes_in[:, pl.ds(at, block)], blank, lanes_in[:, pl.ds(at + block, block)], blank], axis=0
-        )
-        turned = dot_nt(eye, piece)
-        wide[pl.ds(at, block), :] = turned[:, :128]
-        wide[pl.ds(at + block, block), :] = turned[:, 128:]
+        for k in range(WIDEN):
+            at = pl.multiple_of((b * WIDEN + k) * 2 * block, 2 * block)
+            piece = jnp.concatenate(
+                [lanes_in[:, pl.ds(at, block)], blank, lanes_in[:, pl.ds(at + block, block)], blank], axis=0
+            )
+            turned = dot_nt(eye, piece)
+            wide[pl.ds(at, block), :] = turned[:, :128]
+            wide[pl.ds(at + block, block), :] = turned[:, 128:]
         return carry
 
-    lax.fori_loop(0, vocab // (2 * block), widen, 0)
+    lax.fori_loop(0, vocab // (2 * block * WIDEN), widen, 0)
 
     load_counts.wait()
     load_lengths.wait()
@@ -284,6 +286,11 @@
     id_rows = chunk_rows // 128
     places = [table_index // groups + u for u in range(TAKE)]
 
+    def send(j):
+        for n in range(len(steps) - 1):
+            piece_copy(j, n).start()
+        own_copy(j).start()
+
     def chunk(j, carry):
         def take(i, inner):
             for v in range(128 // TAKE):
@@ -294,6 +301,14 @@
             return inner
 
         lax.fori_loop(0, id_rows, take, 0)
+
+        @pl.when(j == 1)
+        def _():
+            for copy in first:
+                copy.wait()
+            for copy in second:
+                copy.start()
+
         for n, (dz, dc) in enumerate(steps):
             g = table_peer(dz, dc)
             for t in range(senders):
@@ -303,17 +318,14 @@
                 taken = rows[pl.ds(start + t * per_sender, cap), :]
                 window[n % 2, t * cap : (t + 1) * cap, :] = jnp.where(slot_iota < filled, taken, 0.0).astype(jnp.bfloat16)
             outgoing[j, n] = dot_nt(fold, window[n % 2]).astype(jnp.bfloat16)
-            if n < len(steps) - 1:
-                piece_copy(j, n).start()
-            else:
-                own_copy(j).start()
 
         @pl.when(j == 0)
         def _():
-            for copy in first:
-                copy.wait()
-            for copy in second:
-                copy.start()
+            send(j)
+
+        @pl.when(j > 1)
+        def _():
+            send(j - 1)
 
         return carry
 
@@ -334,6 +346,7 @@
         out[block_rows(j), :] = content_block(content_in, w_in, w_out, hidden)
 
     content(0)
+    send(CHUNKS - 1)
     for copy in second:
         copy.wait()
     build_caches(cache, keys, vals, lengths[table_index])

time: 73.6 us -> 64.4 us (0.88)
  Pallas kernels: 72.4 us -> 62.6 us
    pallas_call x1, Pallas kernels: 72.4 us -> 62.6 us  [local(): pl.pallas_call(functools.partial(rank_kernel, dims), out_shape=jax.ShapeD...]
where the time goes in v5:
time: 64.4 us; the launch traced here: 63.8 us
  Pallas kernels  62.6 us (97%)
  local copies, waits for them, and re-layouts  1.15 us (2%)
    pallas_call x1, Pallas kernels, local(): pl.pallas_call(functools.partial(rank_kernel, dims), out_shape=jax.ShapeD...  62.6 us

profile of v5, /device:TPU:1, one launch (start us, length us, event | category | flops | bytes accessed | tf_op | source)
XLA Modules:
  0.0 63.8 jit_solution(17554807537414167124)
XLA Ops:
  0.0 62.6 %rank.1 = bf16[1536,512]{1,0:T(8,128)(2,1)S(1)} custom-call(s32[16]{0:T(128)} %lengths_hbm.1, s32[128,128]{1,0:T(8,128)} %bitcast.5, s32[16,16,16]{2,1,0:T(8,128)} %counts_hbm.1, bf16[32,32768]{1,0:T(8,128)(2,1)} %bitcast.3, bf16[2,2,32,512]{3,2,1,0:T(8,128)(2,1)} %bitcast.4, bf16[512,2048]{1,0:T(8,128)(2,1)} %w_in_hbm.1, bf16[2048,512]{1,0:T(8,128)(2,1)} %w_out_hbm.1, ...), custom_call_target="tpu_custom_call" | custom-call | tf_op jit(solution)/shard_map/rank/pallas_call | solution.py:382
  62.6 1.1 %copy.11 = bf16[1536,512]{1,0:T(8,128)(2,1)} copy(bf16[1536,512]{1,0:T(8,128)(2,1)S(1)} %rank.1) | data formatting | bytes 3145728

commit v6 on v5

--- a/solution.py
+++ b/solution.py
@@ -16,7 +16,7 @@
 CHUNKS = 4
 TAKE = 8
 PARTS = 2
-WIDEN = 4
+WIDEN = 16
 NT = (((1,), (1,)), ((), ()))
 
 
@@ -155,6 +155,7 @@
     hidden,
     weights,
     load_sem,
+    table_sem,
     weight_sem,
     piece_send,
     piece_recv,
@@ -182,11 +183,17 @@
 
     mine = pl.ds(y * hist_rows, hist_rows)
     load_ids = pltpu.make_async_copy(ids_hbm, ids_in, load_sem.at[0])
-    load_table = pltpu.make_async_copy(table_hbm, lanes_in, load_sem.at[1])
+    table_part = 512 * WIDEN
+    table_loads = vocab // table_part
+
+    def table_load(c):
+        part = pl.ds(pl.multiple_of(c * table_part, table_part), table_part)
+        return pltpu.make_async_copy(table_hbm.at[:, part], lanes_in.at[:, part], table_sem.at[c])
+
     load_counts = pltpu.make_async_copy(counts_hbm.at[:, shard, :], counts, load_sem.at[2])
     load_hist = pltpu.make_async_copy(hist_hbm, cache.at[:, :, x, mine, :], load_sem.at[3])
     load_lengths = pltpu.make_async_copy(lengths_hbm, lengths, load_sem.at[4])
-    for load in (load_ids, load_table, load_counts, load_hist, load_lengths):
+    for load in (load_ids, load_counts, load_lengths, *map(table_load, range(table_loads)), load_hist):
         load.start()
     sources = (w_in_hbm, w_out_hbm, w_proj_hbm, w_back_hbm)
     targets = (w_in, w_out, w_proj, w_back)
@@ -204,14 +211,23 @@
     ids_low[...] = ids_in[...] & (vocab - 1)
     move_ids = pltpu.make_async_copy(ids_low, ids, load_sem.at[0])
     move_ids.start()
-    load_table.wait()
-    for load in weight_loads:
-        load.start()
+    load_counts.wait()
+    load_lengths.wait()
+
+    def offset_row(t, carry):
+        total = jnp.int32(0)
+        for g in range(groups):
+            offsets[t, g] = total
+            total = total + counts[t, g]
+        return carry
+
+    lax.fori_loop(0, groups, offset_row, 0)
     block = 256
     eye = identity(block, block, jnp.bfloat16)
     blank = jnp.zeros((128 - columns, block), jnp.bfloat16)
 
     def widen(b, carry):
+        table_load(b).wait()
         for k in range(WIDEN):
             at = pl.multiple_of((b * WIDEN + k) * 2 * block, 2 * block)
             piece = jnp.concatenate(
@@ -222,19 +238,10 @@
             wide[pl.ds(at + block, block), :] = turned[:, 128:]
         return carry
 
-    lax.fori_loop(0, vocab // (2 * block * WIDEN), widen, 0)
-
-    load_counts.wait()
-    load_lengths.wait()
-
-    def offset_row(t, carry):
-        total = jnp.int32(0)
-        for g in range(groups):
-            offsets[t, g] = total
-            total = total + counts[t, g]
-        return carry
-
-    lax.fori_loop(0, groups, offset_row, 0)
+    lax.fori_loop(0, table_loads, widen, 0)
+    for load in weight_loads:
+        load.start()
+
     load_hist.wait()
     pl.semaphore_wait(barrier, len(steps) - 1 + len(x_far) + len(y_far))
 
@@ -407,6 +414,7 @@
             vmem((block, w_in.shape[1]), jnp.bfloat16),
             vmem((2, 2, block, hist), jnp.bfloat16),
             dma((5,)),
+            dma((vocab // (512 * WIDEN),)),
             dma((4,)),
             dma((CHUNKS, groups)),
             dma((CHUNKS, groups)),

time: 64.4 us -> 62.2 us (0.966)
  Pallas kernels: 62.6 us -> 61 us
    pallas_call x1, Pallas kernels: 62.6 us -> 61 us  [local(): pl.pallas_call(functools.partial(rank_kernel, dims), out_shape=jax.ShapeD...]
where the time goes in v6:
time: 62.2 us; the launch traced here: 62.1 us
  Pallas kernels  61 us (98%)
  local copies, waits for them, and re-layouts  1.15 us (2%)
    pallas_call x1, Pallas kernels, local(): pl.pallas_call(functools.partial(rank_kernel, dims), out_shape=jax.ShapeD...  61 us

profile of v6, /device:TPU:1, one launch (start us, length us, event | category | flops | bytes accessed | tf_op | source)
XLA Modules:
  0.0 62.1 jit_solution(2835675932505718933)
XLA Ops:
  0.0 61.0 %rank.1 = bf16[1536,512]{1,0:T(8,128)(2,1)S(1)} custom-call(s32[16]{0:T(128)} %lengths_hbm.1, s32[128,128]{1,0:T(8,128)} %bitcast.5, s32[16,16,16]{2,1,0:T(8,128)} %counts_hbm.1, bf16[32,32768]{1,0:T(8,128)(2,1)} %bitcast.3, bf16[2,2,32,512]{3,2,1,0:T(8,128)(2,1)} %bitcast.4, bf16[512,2048]{1,0:T(8,128)(2,1)} %w_in_hbm.1, bf16[2048,512]{1,0:T(8,128)(2,1)} %w_out_hbm.1, ...), custom_call_target="tpu_custom_call" | custom-call | tf_op jit(solution)/shard_map/rank/pallas_call | solution.py:389
  61.0 1.1 %copy.11 = bf16[1536,512]{1,0:T(8,128)(2,1)} copy(bf16[1536,512]{1,0:T(8,128)(2,1)S(1)} %rank.1) | data formatting | bytes 3145728

commit v7 on v6

--- a/solution.py
+++ b/solution.py
@@ -345,15 +345,18 @@
     def block_rows(j):
         return pl.ds(pl.multiple_of(j * chunk_slots, chunk_slots), chunk_slots)
 
-    def content(j):
+    def arrive(j):
         for n in range(len(steps) - 1):
             piece_copy(j, n).wait()
         own_copy(j).wait()
+
+    def content(j):
         content_in = dot_nt(turn, emb[:, block_rows(j)]).astype(jnp.bfloat16)
         out[block_rows(j), :] = content_block(content_in, w_in, w_out, hidden)
 
+    arrive(0)
+    send(CHUNKS - 1)
     content(0)
-    send(CHUNKS - 1)
     for copy in second:
         copy.wait()
     build_caches(cache, keys, vals, lengths[table_index])
@@ -361,6 +364,7 @@
     def run(j, carry):
         @pl.when(j > 0)
         def _():
+            arrive(j)
             content(j)
 
         out[block_rows(j), :] = layers_block(out[block_rows(j), :], w_proj, w_back, keys, vals, weights)

time: 62.2 us -> 62.2 us (level)
  no operation moved by 1% of the time
where the time goes in v7:
time: 62.2 us; the launch traced here: 62.1 us
  Pallas kernels  61 us (98%)
  local copies, waits for them, and re-layouts  1.15 us (2%)
    pallas_call x1, Pallas kernels, local(): pl.pallas_call(functools.partial(rank_kernel, dims), out_shape=jax.ShapeD...  61 us

profile of v7, /device:TPU:1, one launch (start us, length us, event | category | flops | bytes accessed | tf_op | source)
XLA Modules:
  0.0 62.1 jit_solution(7814713103209627572)
XLA Ops:
  0.0 61.0 %rank.1 = bf16[1536,512]{1,0:T(8,128)(2,1)S(1)} custom-call(s32[16]{0:T(128)} %lengths_hbm.1, s32[128,128]{1,0:T(8,128)} %bitcast.5, s32[16,16,16]{2,1,0:T(8,128)} %counts_hbm.1, bf16[32,32768]{1,0:T(8,128)(2,1)} %bitcast.3, bf16[2,2,32,512]{3,2,1,0:T(8,128)(2,1)} %bitcast.4, bf16[512,2048]{1,0:T(8,128)(2,1)} %w_in_hbm.1, bf16[2048,512]{1,0:T(8,128)(2,1)} %w_out_hbm.1, ...), custom_call_target="tpu_custom_call" | custom-call | tf_op jit(solution)/shard_map/rank/pallas_call | solution.py:393
  61.0 1.1 %copy.11 = bf16[1536,512]{1,0:T(8,128)(2,1)} copy(bf16[1536,512]{1,0:T(8,128)(2,1)S(1)} %rank.1) | data formatting | bytes 3145728
